TPU v7x, 32 devices: a whole 2x2x4 slice. The times are simulated.
32 devices in a mesh: row: 8 (over y, x, core), col: 4 (over z).
Axes of the slice: x: 2, y: 2, z: 4, core: 2. Of those that a mesh axis runs over, the one named last changes fastest.
Arguments:
- blocks: bfloat16 [8, 4, 320, 128, 128], P('row', 'col'), may hold values from -0.1875 to 0.1875
- block_rows: int32 [8, 4, 320], P('row', 'col'), may hold values from 0 to 1023, as said below
- block_cols: int32 [8, 4, 320], P('row', 'col'), may hold values from 0 to 1023, as said below
- counts: int32 [8, 4], P('row', 'col'), may hold values from 160 to 320, as said below
- panel: bfloat16 [32, 131072], P(None, ('row', 'col'))
Outputs:
- basis: bfloat16 [32, 131072], P(None, ('row', 'col'))
- factor: float32 [32, 32], replicated
Inputs may be any that keep to these rules, and one draw needn't show every extreme that they name: `block_rows`: split the block-rows into shards of 32 in order; every block of device (r, c) lies in a block-row of a shard whose index modulo 4 is c. Pairs may repeat. `block_cols`: every block of device (r, c) lies in a block-column of a shard whose index divided by 4 is r. `counts`: some device has all 320 slots live.
All inputs are finite; a program needn't handle non-finite values.
Results may differ from a plain program's by a relative error of at most 0.001.
Values may be sent and summed in bfloat16 or wider, within the bound.
No kernel may reach another device: no remote copies, remote signals or barrier semaphores. Data moves between devices by JAX's collectives and lax.ppermute only.
A program may use at most 64 MiB of HBM per device.

v0:
```python
import jax
import jax.numpy as jnp
from jax import lax
from jax.sharding import PartitionSpec as P


def on_device(blocks, block_rows, block_cols, counts, panel):
    width = blocks.shape[-1]
    slot_count = blocks.shape[2]
    panel_cols = panel.shape[0]
    nb_dev = panel.shape[1] // width
    grid_rows = lax.axis_size("row")
    grid_cols = lax.axis_size("col")
    span = nb_dev * grid_cols
    whole = lax.all_gather(panel, "col", axis=1, tiled=True)
    tiles = whole.reshape(panel_cols, span, width)
    global_rows = block_rows[0, 0]
    local_cols = block_cols[0, 0] % span
    local_rows = global_rows // span * nb_dev + global_rows % nb_dev
    live = (jnp.arange(slot_count, dtype=jnp.int32) < counts[0, 0]).astype(jnp.float32)
    picked = jnp.take(tiles, local_cols, axis=1)
    products = jnp.einsum("psk,sjk->spj", picked, blocks[0, 0], preferred_element_type=jnp.float32)
    products = products * live[:, None, None]
    partial_sum = jax.ops.segment_sum(products, local_rows, num_segments=grid_rows * nb_dev)
    owned = lax.psum_scatter(partial_sum, "row", scatter_dimension=0, tiled=True)
    product_t = jnp.transpose(owned, (1, 0, 2)).reshape(panel_cols, nb_dev * width)
    total_rows = nb_dev * width * grid_rows * grid_cols
    local_gram = jnp.dot(
        product_t, product_t.T, precision=lax.Precision.HIGHEST, preferred_element_type=jnp.float32
    )
    gram = lax.psum(local_gram, ("row", "col")) / total_rows
    lower = jnp.linalg.cholesky(gram)
    basis = jax.scipy.linalg.solve_triangular(lower, product_t, lower=True)
    return (basis.astype(jnp.bfloat16), lower.T)


def solution(mesh):
    in_specs = (
        P("row", "col", None, None, None),
        P("row", "col", None),
        P("row", "col", None),
        P("row", "col"),
        P(None, ("row", "col")),
    )
    out_specs = (P(None, ("row", "col")), P())
    return jax.shard_map(
        on_device, mesh=mesh, in_specs=in_specs, out_specs=out_specs, check_vma=False
    )
```

profile of v0, /device:TPU:0, one launch (start us, length us, event | category | flops | bytes accessed | tf_op | source)
XLA Modules:
  0.0 211.6 jit_solution(440297915687399267)
XLA Ops:
  7.2 0.0 all-gather.2.cloned.1.call-start
  7.2 0.7 all-gather.2.cloned.1.call-update
  7.9 0.0 reduce-scatter.2.cloned.1.call-start
  8.6 0.7 reduce.7
  9.3 0.7 fusion.19
  10.0 0.7 fusion.21
  10.7 29.5 %all-gather.2.cloned.1.call-done = bf16[32,16384]{1,0:T(8,128)(2,1)} async-done(((bf16[32,4096]{1,0:T(8,128)(2,1)}), bf16[32,16384]{1,0:T(8,128)(2,1)}) %all-gather.2.cloned.1.call-update) | async-done | bytes 1048592 | tf_op jit(solution)/shard_map/all_gather | solution.py:15
  40.2 1.4 copy_bitcast_fusion
  41.6 3.0 %gather_fusion = bf16[320,32,128]{2,1,0:T(8,128)(2,1)} fusion(bf16[32,128,128]{2,0,1:T(8,128)(2,1)S(1)} %copy_bitcast_fusion, s32[1024]{0:T(1024)S(1)} %pad_clamp_fusion), kind=kCustom, calls=%fused_computation | custom fusion | bytes 5244160 | tf_op jit(solution)/shard_map/jit(_take)/gather | solution.py:21
  44.7 12.7 %broadcast_multiply_fusion = f32[320,32,128]{2,1,0:T(8,128)} fusion(f32[320]{0:T(512)S(1)} %get-tuple-element.10, bf16[1,1,320,128,128]{4,3,2,1,0:T(8,128)(2,1)} %param.5, bf16[320,32,128]{2,1,0:T(8,128)(2,1)} %gather_fusion, pred[320]{0:T(512)(128)(4,1)S(1)} %get-tuple-element.11), kind=kOutput, calls=%fused_computation.7 | convolution fusion | flops 338165760 | bytes 18351680 | tf_op jit(solution)/shard_map/psk,sjk->spj/dot_general | solution.py:22
  57.4 2.5 %broadcast_in_dim.17 = f32[256,32,128]{2,1,0:T(8,128)} broadcast(f32[]{:T(128)} %constant.88.clone.1), dimensions={} | broadcast | bytes 4194308 | tf_op jit(solution)/shard_map/broadcast_in_dim | solution.py:24
  59.9 42.8 %scatter_fusion = f32[256,32,128]{2,1,0:T(8,128)} fusion(f32[256,32,128]{2,1,0:T(8,128)} %broadcast_in_dim.17, s32[320]{0:T(512)S(1)} %fusion.21, f32[320,32,128]{2,1,0:T(8,128)} %broadcast_multiply_fusion), kind=kCustom, calls=%fused_computation.1 | custom fusion | flops 1310720 | bytes 15729920 | tf_op jit(solution)/shard_map/scatter-add | solution.py:24
  102.7 0.0 reduce-scatter.2.cloned.1.call-update
  102.7 51.0 %reduce-scatter.2.cloned.1.call-done = f32[32,32,128]{2,1,0:T(8,128)} async-done(((f32[256,32,128]{2,1,0:T(8,128)}), f32[32,32,128]{2,1,0:T(8,128)}) %reduce-scatter.2.cloned.1.call-update) | async-done | bytes 524304 | tf_op jit(solution)/shard_map/reduce_scatter | solution.py:25
  153.7 1.8 convolution_bitcast_fusion
  155.5 39.4 %psum.7 = f32[32,32]{0,1:T(8,128)S(1)} all-reduce(f32[32,32]{0,1:T(8,128)S(1)} %convolution_bitcast_fusion), channel_id=1, replica_groups=mesh['row'=8,'col'=4] {'row','col'}, use_global_device_ids=true, to_apply=%region_2.3 | all-reduce | flops 1024 | bytes 8192 | tf_op jit(solution)/shard_map/psum | solution.py:31
  194.9 0.1 copy.17
  195.0 2.9 %cholesky.16 = f32[32,32]{1,0:T(8,128)S(1)} custom-call(f32[32,32]{1,0:T(8,128)S(1)} %fusion.14), custom_call_target="Cholesky" | custom-call | tf_op jit(solution)/shard_map/jit(cholesky)/cholesky | solution.py:32
  198.0 0.6 compare_reduce_fusion
  198.6 0.7 fusion.15
  199.3 0.7 copy.19
  199.9 2.4 %custom-call.7 = f32[1,32,32]{1,2,0:T(8,128)S(1)} custom-call(f32[1,32,32]{2,1,0:T(8,128)S(1)} %get-tuple-element.9), custom_call_target="InvertDiagBlocksLowerTriangular" | custom-call | tf_op jit(solution)/shard_map/jit(_solve_triangular)/triangular_solve | solution.py:33
  202.4 2.4 %convolution_convert_fusion = bf16[32,4096]{1,0:T(8,128)(2,1)} fusion(f32[1,32,32]{1,2,0:T(8,128)S(1)} %custom-call.7, f32[32,32,128]{2,1,0:T(8,128)} %reduce-scatter.2.cloned.1.call-done), kind=kOutput, calls=%fused_computation.4 | convolution fusion | flops 50462720 | bytes 790528 | tf_op jit(solution)/shard_map/jit(_solve_triangular)/triangular_solve | solution.py:33
  (5 shorter events, 0.1 us)
Async XLA Ops:
  7.2 33.1 %all-gather.2.cloned.1.call-start = ((), (), s32[]{:S(2)}) async-start(), calls=%async_computation.1 | async-start | bytes 1310720 | tf_op jit(solution)/shard_map/all_gather | solution.py:15
  7.9 145.8 %reduce-scatter.2.cloned.1.call-start = ((), (), s32[]{:S(2)}) async-start(), calls=%async_computation.2 | async-start | bytes 4718592 | tf_op jit(solution)/shard_map/reduce_scatter | solution.py:25
Sparse Core Ops, SparseCore 0:
  9.6 30.6 all-gather.1
  102.9 50.8 reduce-scatter.1
where the time goes:
time: 212 us
  waiting for transfers between devices  81.2 us (38%)
  other arithmetic  51.6 us (24%)
  blocking collectives  39.4 us (19%)
  matrix products  16.8 us (8%)
  between operations  14.7 us (7%)
  local copies, waits for them, and re-layouts  7.72 us (4%)
    reduce_scatter x1, waiting for transfers between devices, on_device(): lax.psum_scatter(partial_sum, 'row', scatter_dimension=0, tiled=True)  51 us
    scatter-add x1, other arithmetic, on_device(): jax.ops.segment_sum(products, local_rows, num_segments=grid_rows * nb_dev)  42.8 us
    psum x1, blocking collectives, on_device(): gram = lax.psum(local_gram, ('row', 'col')) / total_rows  39.4 us
    all_gather x1, waiting for transfers between devices, on_device(): whole = lax.all_gather(panel, 'col', axis=1, tiled=True)  29.5 us
    dot_general x1, matrix products, on_device(): jnp.einsum('psk,sjk->spj', picked, blocks[0, 0], preferred_element_type=j...  12.7 us
  transfers between devices with their start and end apart: 2, of which 2 were waited for; matrix products, arithmetic and copies ran while one was open for 1% of the time, Pallas kernels for 0%

commit v1 on v0

--- a/solution.py
+++ b/solution.py
@@ -12,7 +12,23 @@
     grid_rows = lax.axis_size("row")
     grid_cols = lax.axis_size("col")
     span = nb_dev * grid_cols
-    whole = lax.all_gather(panel, "col", axis=1, tiled=True)
+    size, index, rows = (lax.axis_size("col"), lax.axis_index("col"), panel.shape[1])
+    right = [(i, (i + 1) % size) for i in range(size)]
+    left = [(i, (i - 1) % size) for i in range(size)]
+    whole = jnp.zeros((*panel.shape[:1], size * rows, *panel.shape[1 + 1 :]), panel.dtype)
+    whole = lax.dynamic_update_slice_in_dim(whole, panel, index * rows, axis=1)
+    from_left = from_right = panel
+    half = size // 2
+    for step in range(1, half + 1):
+        from_left = lax.ppermute(from_left, "col", right)
+        whole = lax.dynamic_update_slice_in_dim(
+            whole, from_left, (index - step) % size * rows, axis=1
+        )
+        if step < size - half:
+            from_right = lax.ppermute(from_right, "col", left)
+            whole = lax.dynamic_update_slice_in_dim(
+                whole, from_right, (index + step) % size * rows, axis=1
+            )
     tiles = whole.reshape(panel_cols, span, width)
     global_rows = block_rows[0, 0]
     local_cols = block_cols[0, 0] % span

time: 212 us -> 203 us (0.958)
  waiting for transfers between devices: 81.2 us -> 65.3 us
  starting transfers between devices: 0.08 us -> 6.76 us
    all_gather x1 -> x0, waiting for transfers between devices: 29.5 us -> none  [on_device(): whole = lax.all_gather(panel, 'col', axis=1, tiled=True)]
    ppermute x0 -> x3, waiting for transfers between devices: none -> 15.6 us  [the longest x2 15.6 us: on_device(): from_left = lax.ppermute(from_left, 'col', right)]
    ppermute x0 -> x3, starting transfers between devices: none -> 6.73 us  [the longest x1 5.1 us: on_device(): from_right = lax.ppermute(from_right, 'col', left)]
  transfers between devices with their start and end apart: 2 -> 4, of which waited for: 2 -> 3; matrix products, arithmetic and copies ran while one was open for 1% -> 2% of each run, Pallas kernels for 0% -> 0%
where the time goes in v1:
time: 203 us; the launch traced here: 202 us
  waiting for transfers between devices  65.3 us (32%)
  other arithmetic  51.6 us (25%)
  blocking collectives  39.4 us (19%)
  matrix products  16.9 us (8%)
  between operations  14.8 us (7%)
  local copies, waits for them, and re-layouts  7.61 us (4%)
  starting transfers between devices  6.76 us (3%)
    reduce_scatter x1, waiting for transfers between devices, on_device(): lax.psum_scatter(partial_sum, 'row', scatter_dimension=0, tiled=True)  49.7 us
    scatter-add x1, other arithmetic, on_device(): jax.ops.segment_sum(products, local_rows, num_segments=grid_rows * nb_dev)  42.8 us
    psum x1, blocking collectives, on_device(): gram = lax.psum(local_gram, ('row', 'col')) / total_rows  39.4 us
    ppermute x2, waiting for transfers between devices, on_device(): from_left = lax.ppermute(from_left, 'col', right)  15.6 us
    dot_general x1, matrix products, on_device(): jnp.einsum('psk,sjk->spj', picked, blocks[0, 0], preferred_element_type=j...  12.7 us
    ppermute x1, starting transfers between devices, on_device(): from_right = lax.ppermute(from_right, 'col', left)  5.1 us
  transfers between devices with their start and end apart: 4, of which 3 were waited for; matrix products, arithmetic and copies ran while one was open for 2% of the time, Pallas kernels for 0%

profile of v1, /device:TPU:0, one launch (start us, length us, event | category | flops | bytes accessed | tf_op | source)
XLA Modules:
  0.0 202.4 jit_solution(2956414949260222491)
XLA Ops:
  7.2 0.0 reduce-scatter.2.cloned.1.call-start
  7.2 5.1 %collective-permute-start.1 = (bf16[32,4096]{1,0:T(8,128)(2,1)}, bf16[32,4096]{1,0:T(8,128)(2,1)S(1)}, u32[]{:S(2)}, u32[]{:S(2)}) collective-permute-start(bf16[32,4096]{1,0:T(8,128)(2,1)} %param.9), channel_id=1, source_target_pairs={{0,3},{1,0},{2,1},{3,2},{4,7},{5,4},{6,5},{7,6},{8,11},{9,8},{10,9... | collective-permute-start | bytes 786440 | tf_op jit(solution)/shard_map/ppermute | solution.py:28
  12.3 0.0 collective-permute-start
  12.3 0.7 fusion.21
  13.0 0.7 fusion.19
  13.7 0.1 broadcast_in_dim.22
  13.8 1.0 constant_dynamic-update-slice_fusion.3
  14.9 0.7 reduce.7
  16.2 8.4 %collective-permute-done = bf16[32,4096]{1,0:T(8,128)(2,1)S(1)} collective-permute-done((bf16[32,4096]{1,0:T(8,128)(2,1)}, bf16[32,4096]{1,0:T(8,128)(2,1)S(1)}, u32[]{:S(2)}, u32[]{:S(2)}) %collective-permute-start) | collective-permute-done | bytes 262176 | tf_op jit(solution)/shard_map/ppermute | solution.py:23
  24.6 1.6 collective-permute-start.2
  26.3 0.0 collective-permute-done.1
  26.3 7.3 %collective-permute-done.2 = bf16[32,4096]{1,0:T(8,128)(2,1)S(1)} collective-permute-done((bf16[32,4096]{1,0:T(8,128)(2,1)S(1)}, bf16[32,4096]{1,0:T(8,128)(2,1)S(1)}, u32[]{:S(2)}, u32[]{:S(2)}) %collective-permute-start.2) | collective-permute-done | bytes 262176 | tf_op jit(solution)/shard_map/ppermute | solution.py:23
  33.6 0.2 copy_bitcast_fusion
  33.8 3.0 %gather_fusion = bf16[320,32,128]{2,1,0:T(8,128)(2,1)} fusion(bf16[32,128,128]{2,0,1:T(8,128)(2,1)S(1)} %copy_bitcast_fusion, s32[1024]{0:T(1024)S(1)} %pad_clamp_fusion), kind=kCustom, calls=%fused_computation | custom fusion | bytes 5244160 | tf_op jit(solution)/shard_map/jit(_take)/gather | solution.py:37
  36.8 12.7 %broadcast_multiply_fusion = f32[320,32,128]{2,1,0:T(8,128)} fusion(f32[320]{0:T(512)S(1)} %get-tuple-element.10, bf16[1,1,320,128,128]{4,3,2,1,0:T(8,128)(2,1)} %param.5, bf16[320,32,128]{2,1,0:T(8,128)(2,1)} %gather_fusion, pred[320]{0:T(512)(128)(4,1)S(1)} %get-tuple-element.11), kind=kOutput, calls=%fused_computation.7 | convolution fusion | flops 338165760 | bytes 18351680 | tf_op jit(solution)/shard_map/psk,sjk->spj/dot_general | solution.py:38
  49.5 2.5 %broadcast_in_dim.20 = f32[256,32,128]{2,1,0:T(8,128)} broadcast(f32[]{:T(128)} %constant.117.clone.1), dimensions={} | broadcast | bytes 4194308 | tf_op jit(solution)/shard_map/broadcast_in_dim | solution.py:40
  52.1 42.8 %scatter_fusion = f32[256,32,128]{2,1,0:T(8,128)} fusion(f32[256,32,128]{2,1,0:T(8,128)} %broadcast_in_dim.20, s32[320]{0:T(512)S(1)} %fusion.21, f32[320,32,128]{2,1,0:T(8,128)} %broadcast_multiply_fusion), kind=kCustom, calls=%fused_computation.1 | custom fusion | flops 1310720 | bytes 15729920 | tf_op jit(solution)/shard_map/scatter-add | solution.py:40
  94.9 0.0 reduce-scatter.2.cloned.1.call-update
  94.9 49.7 %reduce-scatter.2.cloned.1.call-done = f32[32,32,128]{2,1,0:T(8,128)} async-done(((f32[256,32,128]{2,1,0:T(8,128)}), f32[32,32,128]{2,1,0:T(8,128)}) %reduce-scatter.2.cloned.1.call-update) | async-done | bytes 524304 | tf_op jit(solution)/shard_map/reduce_scatter | solution.py:41
  144.5 1.8 convolution_bitcast_fusion
  146.3 39.4 %psum.7 = f32[32,32]{0,1:T(8,128)S(1)} all-reduce(f32[32,32]{0,1:T(8,128)S(1)} %convolution_bitcast_fusion), channel_id=1, replica_groups=mesh['row'=8,'col'=4] {'row','col'}, use_global_device_ids=true, to_apply=%region_2.3 | all-reduce | flops 1024 | bytes 8192 | tf_op jit(solution)/shard_map/psum | solution.py:47
  185.7 0.1 copy.17
  185.8 2.9 %cholesky.16 = f32[32,32]{1,0:T(8,128)S(1)} custom-call(f32[32,32]{1,0:T(8,128)S(1)} %fusion.14), custom_call_target="Cholesky" | custom-call | tf_op jit(solution)/shard_map/jit(cholesky)/cholesky | solution.py:48
  188.8 0.6 compare_reduce_fusion
  189.4 0.7 fusion.15
  190.1 0.7 copy.19
  190.8 2.4 %custom-call.7 = f32[1,32,32]{1,2,0:T(8,128)S(1)} custom-call(f32[1,32,32]{2,1,0:T(8,128)S(1)} %get-tuple-element.9), custom_call_target="InvertDiagBlocksLowerTriangular" | custom-call | tf_op jit(solution)/shard_map/jit(_solve_triangular)/triangular_solve | solution.py:49
  193.2 2.4 %convolution_convert_fusion = bf16[32,4096]{1,0:T(8,128)(2,1)} fusion(f32[1,32,32]{1,2,0:T(8,128)S(1)} %custom-call.7, f32[32,32,128]{2,1,0:T(8,128)} %reduce-scatter.2.cloned.1.call-done), kind=kOutput, calls=%fused_computation.4 | convolution fusion | flops 50462720 | bytes 790528 | tf_op jit(solution)/shard_map/jit(_solve_triangular)/triangular_solve | solution.py:49
  (8 shorter events, 0.1 us)
Async XLA Ops:
  7.2 137.4 %reduce-scatter.2.cloned.1.call-start = ((), (), s32[]{:S(2)}) async-start(), calls=%async_computation.1 | async-start | bytes 4718592 | tf_op jit(solution)/shard_map/reduce_scatter | solution.py:41
  7.2 19.0 %collective-permute-start.1 = (bf16[32,4096]{1,0:T(8,128)(2,1)}, bf16[32,4096]{1,0:T(8,128)(2,1)S(1)}, u32[]{:S(2)}, u32[]{:S(2)}) collective-permute-start(bf16[32,4096]{1,0:T(8,128)(2,1)} %param.9), channel_id=1, source_target_pairs={{0,3},{1,0},{2,1},{3,2},{4,7},{5,4},{6,5},{7,6},{8,11},{9,8},{10,9... | collective-permute-start | bytes 786440 | tf_op jit(solution)/shard_map/ppermute | solution.py:28
  12.3 12.3 %collective-permute-start = (bf16[32,4096]{1,0:T(8,128)(2,1)}, bf16[32,4096]{1,0:T(8,128)(2,1)S(1)}, u32[]{:S(2)}, u32[]{:S(2)}) collective-permute-start(bf16[32,4096]{1,0:T(8,128)(2,1)} %param.9), channel_id=1, source_target_pairs={{0,1},{1,2},{2,3},{3,0},{4,5},{5,6},{6,7},{7,4},{8,9},{9,10},{10,1... | collective-permute-start | bytes 786440 | tf_op jit(solution)/shard_map/ppermute | solution.py:23
  24.6 9.0 %collective-permute-start.2 = (bf16[32,4096]{1,0:T(8,128)(2,1)S(1)}, bf16[32,4096]{1,0:T(8,128)(2,1)S(1)}, u32[]{:S(2)}, u32[]{:S(2)}) collective-permute-start(bf16[32,4096]{1,0:T(8,128)(2,1)S(1)} %collective-permute-done), channel_id=1, source_target_pairs={{0,1},{1,2},{2,3},{3,0},{4,5},{5,6},{6,7},{7,4},{8,9},{9,10},{10,1... | collective-permute-start | bytes 786440 | tf_op jit(solution)/shard_map/ppermute | solution.py:23
Sparse Core Ops, SparseCore 0:
  95.0 49.4 reduce-scatter.1

commit v2 on v0

--- a/solution.py
+++ b/solution.py
@@ -28,7 +28,7 @@
     local_gram = jnp.dot(
         product_t, product_t.T, precision=lax.Precision.HIGHEST, preferred_element_type=jnp.float32
     )
-    gram = lax.psum(local_gram, ("row", "col")) / total_rows
+    gram = jnp.sum(lax.all_gather(local_gram, ("row", "col")), 0) / total_rows
     lower = jnp.linalg.cholesky(gram)
     basis = jax.scipy.linalg.solve_triangular(lower, product_t, lower=True)
     return (basis.astype(jnp.bfloat16), lower.T)

time: 212 us -> 244 us (1.15)
  blocking collectives: 39.4 us -> 71.1 us
    all_gather x0 -> x1, blocking collectives: none -> 71.1 us  [on_device(): gram = jnp.sum(lax.all_gather(local_gram, ('row', 'col')), 0) / total_rows]
    psum x1 -> x0, blocking collectives: 39.4 us -> none  [on_device(): gram = lax.psum(local_gram, ('row', 'col')) / total_rows]
where the time goes in v2:
time: 244 us; the launch traced here: 243 us
  waiting for transfers between devices  81.2 us (33%)
  blocking collectives  71.1 us (29%)
  other arithmetic  51.7 us (21%)
  matrix products  16.9 us (7%)
  between operations  14.7 us (6%)
  local copies, waits for them, and re-layouts  7.72 us (3%)
    all_gather x1, blocking collectives, on_device(): gram = jnp.sum(lax.all_gather(local_gram, ('row', 'col')), 0) / total_rows  71.1 us
    reduce_scatter x1, waiting for transfers between devices, on_device(): lax.psum_scatter(partial_sum, 'row', scatter_dimension=0, tiled=True)  51 us
    scatter-add x1, other arithmetic, on_device(): jax.ops.segment_sum(products, local_rows, num_segments=grid_rows * nb_dev)  42.8 us
    all_gather x1, waiting for transfers between devices, on_device(): whole = lax.all_gather(panel, 'col', axis=1, tiled=True)  29.5 us
    dot_general x1, matrix products, on_device(): jnp.einsum('psk,sjk->spj', picked, blocks[0, 0], preferred_element_type=j...  12.7 us
  transfers between devices with their start and end apart: 2, of which 2 were waited for; matrix products, arithmetic and copies ran while one was open for 1% of the time, Pallas kernels for 0%

profile of v2, /device:TPU:0, one launch (start us, length us, event | category | flops | bytes accessed | tf_op | source)
XLA Modules:
  0.0 243.3 jit_solution(12116223484282675301)
XLA Ops:
  7.2 0.0 all-gather.3.cloned.1.call-start
  7.2 0.7 all-gather.3.cloned.1.call-update
  7.9 0.0 reduce-scatter.2.cloned.1.call-start
  8.6 0.7 reduce.7
  9.3 0.7 fusion.19
  10.0 0.7 fusion.21
  10.7 29.5 %all-gather.3.cloned.1.call-done = bf16[32,16384]{1,0:T(8,128)(2,1)} async-done(((bf16[32,4096]{1,0:T(8,128)(2,1)}), bf16[32,16384]{1,0:T(8,128)(2,1)}) %all-gather.3.cloned.1.call-update) | async-done | bytes 1048592 | tf_op jit(solution)/shard_map/all_gather | solution.py:15
  40.2 1.4 copy_bitcast_fusion
  41.6 3.0 %gather_fusion = bf16[320,32,128]{2,1,0:T(8,128)(2,1)} fusion(bf16[32,128,128]{2,0,1:T(8,128)(2,1)S(1)} %copy_bitcast_fusion, s32[1024]{0:T(1024)S(1)} %pad_clamp_fusion), kind=kCustom, calls=%fused_computation | custom fusion | bytes 5244160 | tf_op jit(solution)/shard_map/jit(_take)/gather | solution.py:21
  44.7 12.7 %broadcast_multiply_fusion = f32[320,32,128]{2,1,0:T(8,128)} fusion(f32[320]{0:T(512)S(1)} %get-tuple-element.12, bf16[1,1,320,128,128]{4,3,2,1,0:T(8,128)(2,1)} %param.5, bf16[320,32,128]{2,1,0:T(8,128)(2,1)} %gather_fusion, pred[320]{0:T(512)(128)(4,1)S(1)} %get-tuple-element.13), kind=kOutput, calls=%fused_computation.7 | convolution fusion | flops 338165760 | bytes 18351680 | tf_op jit(solution)/shard_map/psk,sjk->spj/dot_general | solution.py:22
  57.4 2.5 %broadcast_in_dim.17 = f32[256,32,128]{2,1,0:T(8,128)} broadcast(f32[]{:T(128)} %constant.90.clone.1), dimensions={} | broadcast | bytes 4194308 | tf_op jit(solution)/shard_map/broadcast_in_dim | solution.py:24
  59.9 42.8 %scatter_fusion = f32[256,32,128]{2,1,0:T(8,128)} fusion(f32[256,32,128]{2,1,0:T(8,128)} %broadcast_in_dim.17, s32[320]{0:T(512)S(1)} %fusion.21, f32[320,32,128]{2,1,0:T(8,128)} %broadcast_multiply_fusion), kind=kCustom, calls=%fused_computation.1 | custom fusion | flops 1310720 | bytes 15729920 | tf_op jit(solution)/shard_map/scatter-add | solution.py:24
  102.7 0.0 reduce-scatter.2.cloned.1.call-update
  102.7 51.0 %reduce-scatter.2.cloned.1.call-done = f32[32,32,128]{2,1,0:T(8,128)} async-done(((f32[256,32,128]{2,1,0:T(8,128)}), f32[32,32,128]{2,1,0:T(8,128)}) %reduce-scatter.2.cloned.1.call-update) | async-done | bytes 524304 | tf_op jit(solution)/shard_map/reduce_scatter | solution.py:25
  153.7 1.8 convolution_bitcast_fusion
  155.5 71.1 %all-gather = f32[1024,32]{1,0:T(8,128)S(1)} all-gather(f32[32,32]{1,0:T(8,128)S(1)} %convolution_bitcast_fusion), channel_id=2, replica_groups=mesh['row'=8,'col'=4] {'row','col'}, dimensions={0}, use_global_device_ids=true | all-gather | bytes 135168 | tf_op jit(solution)/shard_map/all_gather | solution.py:31
  226.6 0.1 reduce_sum.11
  226.7 0.1 copy.18
  226.7 2.9 %cholesky.16 = f32[32,32]{1,0:T(8,128)S(1)} custom-call(f32[32,32]{1,0:T(8,128)S(1)} %fusion.14), custom_call_target="Cholesky" | custom-call | tf_op jit(solution)/shard_map/jit(cholesky)/cholesky | solution.py:32
  229.7 0.6 compare_reduce_fusion
  230.3 0.7 fusion.15
  231.0 0.7 copy.20
  231.7 2.4 %custom-call.7 = f32[1,32,32]{1,2,0:T(8,128)S(1)} custom-call(f32[1,32,32]{2,1,0:T(8,128)S(1)} %get-tuple-element.11), custom_call_target="InvertDiagBlocksLowerTriangular" | custom-call | tf_op jit(solution)/shard_map/jit(_solve_triangular)/triangular_solve | solution.py:33
  234.1 2.4 convolution_convert_fusion
  (4 shorter events, 0.1 us)
Async XLA Ops:
  7.2 33.1 %all-gather.3.cloned.1.call-start = ((), (), s32[]{:S(2)}) async-start(), calls=%async_computation.1 | async-start | bytes 1310720 | tf_op jit(solution)/shard_map/all_gather | solution.py:15
  7.9 145.8 %reduce-scatter.2.cloned.1.call-start = ((), (), s32[]{:S(2)}) async-start(), calls=%async_computation.2 | async-start | bytes 4718592 | tf_op jit(solution)/shard_map/reduce_scatter | solution.py:25
Sparse Core Ops, SparseCore 0:
  9.6 30.6 all-gather.2
  102.9 50.8 reduce-scatter.1
